TPU v7x, 32 devices: a whole 2x2x4 slice. The times are simulated.
32 devices in a mesh: band: 4 (over y, core), pgroup: 8 (over z, x).
Axes of the slice: x: 2, y: 2, z: 4, core: 2. Of those that a mesh axis runs over, the one named last changes fastest.
Arguments:
- state: float32 [128, 256, 512], P('pgroup', 'band'), may hold values from -6 to 6
- forcing: float32 [256, 512], P('band'), may hold values from -3 to 3
- parents: int32 [64, 128], P('band'), may hold values from 0 to 127, as said below
- taper_index: int32 [256], P('band'), may hold values from 0 to 7
Outputs:
- analysis: float32 [128, 256, 512], P('pgroup', 'band')
Inputs may be any that keep to these rules, and one draw needn't show every extreme that they name: In every patch, the parents of the 16 particles k with k // 16 = g are distinct and come from exactly 8 groups (a group holds the particles j with the same j // 16), exactly 2 from each of them, for every patch and every g.
All inputs are finite; a program needn't handle non-finite values.
Results may differ from a plain program's by a relative error of at most 0.000071.
Values sent between devices are 32-bit elements; how exact they have to be, the bound alone decides.
A program may use at most 64 MiB of HBM per device.

v0:
```python
import functools

import jax
import jax.numpy as jnp
from jax import lax
from jax.experimental import pallas as pl
from jax.experimental.pallas import tpu as pltpu
from jax.sharding import PartitionSpec as P

PATCH_ROWS = 4
STEPS = 6
CAP = 2
TILE = 8
MESH = pl.DeviceIdType.MESH


def advance(v, drive, above_ok, below_ok):
    rows, width = v.shape
    v = zero_outside(v, above_ok, below_ok)
    for _ in range(STEPS):
        east = pltpu.roll(v, width - 1, 1)
        west = pltpu.roll(v, 1, 1)
        north = pltpu.roll(v, rows - 1, 0)
        south = pltpu.roll(v, 1, 0)
        v = (
            v * (0.4 - 0.05 * (east - west))
            + (0.15 * (east + west) + drive)
            + (0.05 * north + 0.25 * south)
        )
        v = zero_outside(v, above_ok, below_ok)
    return v


def zero_outside(v, above_ok, below_ok):
    if above_ok is not None:
        v = jnp.concatenate([jnp.where(above_ok, v[:TILE], 0.0), v[TILE:]], axis=0)
    if below_ok is not None:
        v = jnp.concatenate([v[:-TILE], jnp.where(below_ok, v[-TILE:], 0.0)], axis=0)
    return v


def window(low, mid, high, pick, start, rows):
    extent = mid.shape[-2]
    begin, end = start - TILE, start + rows + TILE
    parts = []
    if begin < 0:
        parts.append(low[pick + (slice(None), slice(None))])
    parts.append(mid[pick + (slice(max(begin, 0), min(end, extent)), slice(None))])
    if end > extent:
        parts.append(high[pick + (slice(None), slice(None))])
    return jnp.concatenate(parts, axis=0) if len(parts) > 1 else parts[0]


def kernel(
    bands, groups, chunks, jobs1, jobs2,
    state, forcing, taper, chosen, picks, out,
    first, resampled,
    s_lo, s_hi, f_lo, f_hi, t_lo, t_hi, r_lo, r_hi,
    halo_send, halo_recv, send_sem, recv_sem, own_sem,
    *buffers,
):
    count = len(chunks)
    sends, recvs = buffers[:count], buffers[count:]
    band = lax.axis_index("band")
    me = lax.axis_index("pgroup")
    per_dev, extent, width = state.shape
    has_low, has_high = band > 0, band < bands - 1
    up, down = lax.rem(band + 1, bands), lax.rem(band + bands - 1, bands)

    barrier = pltpu.get_barrier_semaphore()
    for step in range(1, groups):
        pl.semaphore_signal(
            barrier, inc=1, device_id={"pgroup": lax.rem(me + step, groups)}, device_id_type=MESH
        )

    @pl.when(has_low)
    def _():
        pl.semaphore_signal(barrier, inc=1, device_id={"band": down}, device_id_type=MESH)

    @pl.when(has_high)
    def _():
        pl.semaphore_signal(barrier, inc=1, device_id={"band": up}, device_id_type=MESH)

    def halo(index, src, low, high):
        lead = (slice(None),) * (len(src.shape) - 2)
        upward = pltpu.make_async_remote_copy(
            src_ref=src.at[lead + (slice(extent - TILE, extent),)], dst_ref=low,
            send_sem=halo_send.at[2 * index], recv_sem=halo_recv.at[2 * index],
            device_id={"band": up}, device_id_type=MESH,
        )
        downward = pltpu.make_async_remote_copy(
            src_ref=src.at[lead + (slice(0, TILE),)], dst_ref=high,
            send_sem=halo_send.at[2 * index + 1], recv_sem=halo_recv.at[2 * index + 1],
            device_id={"band": down}, device_id_type=MESH,
        )
        return upward, downward

    edges = [
        halo(0, state, s_lo, s_hi),
        halo(1, forcing, f_lo, f_hi),
        halo(2, taper, t_lo, t_hi),
    ]
    middle = halo(3, resampled, r_lo, r_hi)

    @pl.when(jnp.logical_not(has_low))
    def _():
        for ref in (s_lo, f_lo, t_lo, r_lo):
            ref[...] = jnp.zeros_like(ref)

    @pl.when(jnp.logical_not(has_high))
    def _():
        for ref in (s_hi, f_hi, t_hi, r_hi):
            ref[...] = jnp.zeros_like(ref)

    def bounds(start, rows):
        return (
            has_low if start < TILE else None,
            has_high if start + rows + TILE > extent else None,
        )

    def before(start, rows):
        above_ok, below_ok = bounds(start, rows)

        def body(k, carry):
            v = window(s_lo, state, s_hi, (k,), start, rows)
            drive = window(f_lo, forcing, f_hi, (), start, rows)
            v = advance(v, drive, above_ok, below_ok)
            first[k, pl.ds(start, rows), :] = v[TILE : TILE + rows]
            return carry

        lax.fori_loop(0, per_dev, body, 0)

    def after(start, rows):
        above_ok, below_ok = bounds(start, rows)
        kind = window(t_lo, taper, t_hi, (), start, rows) + 1.0
        near, far = jnp.exp(-0.2 * kind), jnp.exp(-0.8 * kind)
        scale = 1.0 / (1.0 + 2.0 * near + 2.0 * far)
        repeat = width // taper.shape[1]
        w0, w1, w2 = (
            jnp.concatenate([w] * repeat, axis=1) for w in (scale, near * scale, far * scale)
        )

        def body(k, carry):
            v = window(r_lo, resampled, r_hi, (k,), start, rows)
            full = v.shape[0]
            drive = window(f_lo, forcing, f_hi, (), start, rows)
            v = (
                w0 * v
                + w1 * (pltpu.roll(v, 1, 0) + pltpu.roll(v, full - 1, 0))
                + w2 * (pltpu.roll(v, 2, 0) + pltpu.roll(v, full - 2, 0))
            )
            v = advance(v, drive, above_ok, below_ok)
            out[k, pl.ds(start, rows), :] = v[TILE : TILE + rows]
            return carry

        lax.fori_loop(0, per_dev, body, 0)

    shifts = sorted(range(1, groups), key=lambda i: -min(i, groups - i))

    def exchange(index):
        copies = []
        for shift in shifts:
            copies.append(
                pltpu.make_async_remote_copy(
                    src_ref=sends[index].at[lax.rem(me + shift, groups)],
                    dst_ref=recvs[index].at[me],
                    send_sem=send_sem.at[index, shift - 1],
                    recv_sem=recv_sem.at[index, shift - 1],
                    device_id={"pgroup": lax.rem(me + shift, groups)},
                    device_id_type=MESH,
                )
            )
        own = pltpu.make_async_copy(sends[index].at[me], recvs[index].at[me], own_sem.at[index])
        return copies, own

    upper = lax.broadcasted_iota(jnp.int32, (TILE, width), 0) < PATCH_ROWS

    def gather(index):
        base, tiles = chunks[index]
        send = sends[index]

        def body(g, carry):
            for j in range(tiles):
                rows = pl.ds((base + j) * TILE, TILE)
                for slot in range(CAP):
                    at = ((2 * (base + j)) * groups + g) * CAP + slot
                    even, odd = chosen[at], chosen[at + groups * CAP]
                    send[g, j, slot] = jnp.where(upper, first[even, rows, :], first[odd, rows, :])
            return carry

        lax.fori_loop(0, groups, body, 0)

    def scatter(index):
        base, tiles = chunks[index]
        recv = recvs[index]

        def body(k, carry):
            for j in range(tiles):
                at = ((2 * (base + j)) * per_dev + k) * 2
                even = recv[picks[at], j, picks[at + 1]]
                odd = recv[picks[at + 2 * per_dev], j, picks[at + 2 * per_dev + 1]]
                resampled[k, pl.ds((base + j) * TILE, TILE), :] = jnp.where(upper, even, odd)
            return carry

        lax.fori_loop(0, per_dev, body, 0)

    plans = [exchange(index) for index in range(count)]
    for index in range(count):
        for start, rows in jobs1[index]:
            before(start, rows)
        gather(index)
        if index == 0:
            pl.semaphore_wait(
                barrier, groups - 1 + has_low.astype(jnp.int32) + has_high.astype(jnp.int32)
            )

            @pl.when(has_high)
            def _():
                for upward, _ in edges:
                    upward.start()

            @pl.when(has_low)
            def _():
                for _, downward in edges:
                    downward.start()

        copies, own = plans[index]
        for copy in copies:
            copy.start()
        own.start()
        if index == 0:

            @pl.when(has_low)
            def _():
                for upward, _ in edges:
                    upward.wait_recv()

            @pl.when(has_high)
            def _():
                for _, downward in edges:
                    downward.wait_recv()

    for index in range(count):
        copies, own = plans[index]
        for copy in copies:
            copy.wait_recv()
        own.wait()
        scatter(index)
        base, tiles = chunks[index]
        if base == 0:

            @pl.when(has_low)
            def _():
                middle[1].start()

        if (base + tiles) * TILE == extent:

            @pl.when(has_high)
            def _():
                middle[0].start()

        for start, rows in jobs2[index]:
            if start < TILE:

                @pl.when(has_low)
                def _():
                    middle[0].wait_recv()

            if start + rows + TILE > extent:

                @pl.when(has_high)
                def _():
                    middle[1].wait_recv()

            after(start, rows)

    @pl.when(has_high)
    def _():
        for upward, _ in edges:
            upward.wait_send()
        middle[0].wait_send()

    @pl.when(has_low)
    def _():
        for _, downward in edges:
            downward.wait_send()
        middle[1].wait_send()

    for copies, _ in plans:
        for copy in copies:
            copy.wait_send()


def on_device(state, forcing, parents, taper_index):
    per_dev, extent, width = state.shape
    patch_dev = extent // PATCH_ROWS
    bands, groups = lax.axis_size("band"), lax.axis_size("pgroup")
    me = lax.axis_index("pgroup")
    lanes = 128

    table = parents.reshape(patch_dev, groups, per_dev)
    within = table - me * per_dev
    mine = (within >= 0) & (within < per_dev)
    least = jnp.min(jnp.where(mine, within, per_dev - 1), axis=2)
    most = jnp.max(jnp.where(mine, within, 0), axis=2)
    chosen = jnp.stack([least, most], axis=2).reshape(-1)
    own = lax.dynamic_index_in_dim(table, me, 1, keepdims=False)
    source = own // per_dev
    other = (source[:, :, None] == source[:, None, :]) & (own[:, None, :] < own[:, :, None])
    rank = jnp.any(other, axis=2).astype(jnp.int32)
    picks = jnp.stack([source, rank], axis=2).reshape(-1)
    taper = jnp.broadcast_to(taper_index.astype(jnp.float32)[:, None], (extent, lanes))

    quarter = extent // TILE // 4
    part = quarter * TILE
    chunks = [(quarter, quarter), (0, quarter), (3 * quarter, quarter), (2 * quarter, quarter)]
    jobs1 = [[(base * TILE, part)] for base, _ in chunks]
    jobs2 = [
        [],
        [],
        [(0, part), (part, part - TILE), (4 * part - TILE, TILE)],
        [(2 * part - TILE, part), (3 * part - TILE, part)],
    ]
    f32 = jnp.float32
    edge = (per_dev, TILE, width)
    buffers = [
        pltpu.VMEM((groups, tiles, CAP, TILE, width), f32) for _, tiles in chunks
    ]
    vmem, smem = pl.BlockSpec(memory_space=pltpu.VMEM), pl.BlockSpec(memory_space=pltpu.SMEM)
    return pl.pallas_call(
        functools.partial(kernel, bands, groups, chunks, jobs1, jobs2),
        out_shape=jax.ShapeDtypeStruct(state.shape, f32),
        in_specs=[vmem, vmem, vmem, smem, smem],
        out_specs=vmem,
        scratch_shapes=[
            pltpu.VMEM(state.shape, f32),
            pltpu.VMEM(state.shape, f32),
            pltpu.VMEM(edge, f32),
            pltpu.VMEM(edge, f32),
            pltpu.VMEM((TILE, width), f32),
            pltpu.VMEM((TILE, width), f32),
            pltpu.VMEM((TILE, lanes), f32),
            pltpu.VMEM((TILE, lanes), f32),
            pltpu.VMEM(edge, f32),
            pltpu.VMEM(edge, f32),
            pltpu.SemaphoreType.DMA((8,)),
            pltpu.SemaphoreType.DMA((8,)),
            pltpu.SemaphoreType.DMA((len(chunks), groups - 1)),
            pltpu.SemaphoreType.DMA((len(chunks), groups - 1)),
            pltpu.SemaphoreType.DMA((len(chunks),)),
            *buffers,
            *buffers,
        ],
        compiler_params=pltpu.CompilerParams(
            collective_id=0, has_side_effects=True, vmem_limit_bytes=56 << 20
        ),
        name="filter_step",
    )(state, forcing, taper, chosen, picks)


def solution(mesh):
    return jax.shard_map(
        on_device,
        mesh=mesh,
        in_specs=(P("pgroup", "band", None), P("band", None), P("band", None), P("band")),
        out_specs=P("pgroup", "band", None),
        check_vma=False,
    )
```

profile of v0, /device:TPU:14, one launch (start us, length us, event | category | flops | bytes accessed | tf_op | source)
XLA Modules:
  0.0 111.4 jit_solution(14359677218624880476)
XLA Ops:
  0.0 0.7 convert_element_type.16
  0.7 0.7 broadcast_in_dim.7.taper
  1.4 0.8 reshape.95
  2.1 0.1 and_select_fusion
  2.2 0.6 select_reduce_fusion.1
  2.8 0.1 copy.14
  2.9 0.1 copy.15
  3.0 0.5 and_reduce_fusion
  3.5 0.1 copy.16
  3.6 0.7 reshape.96.chosen
  4.3 0.2 copy.17
  4.5 0.7 reshape.97.picks
  5.2 103.1 %filter_step.1 = f32[16,64,512]{2,1,0:T(8,128)} custom-call(f32[16,64,512]{2,1,0:T(8,128)} %state.1, f32[64,512]{1,0:T(8,128)} %forcing.1, f32[64,128]{1,0:T(8,128)} %broadcast_in_dim.7.taper, s32[256]{0:T(256)} %reshape.96.chosen, s32[512]{0:T(512)} %reshape.97.picks), custom_call_target="tpu_custom_call" | custom-call | tf_op jit(solution)/shard_map/filter_step/pallas_call | solution.py:330
  108.3 3.1 %copy.19 = f32[16,64,512]{2,1,0:T(8,128)} copy(f32[16,64,512]{2,1,0:T(8,128)} %filter_step.1) | data formatting | bytes 4194304
  (5 shorter events, 0.0 us)
where the time goes:
time: 112 us; the launch traced here: 111 us
  Pallas kernels  103 us (92%)
  local copies, waits for them, and re-layouts  6.5 us (6%)
  other arithmetic  1.82 us (2%)
    pallas_call x1, Pallas kernels, on_device(): pl.pallas_call(functools.partial(kernel, bands, groups, chunks, jobs1, jo...  103 us
    unnamed x1, local copies, waits for them, and re-layouts  3.14 us

commit v1 on v0

--- a/solution.py
+++ b/solution.py
@@ -10,51 +10,25 @@
 PATCH_ROWS = 4
 STEPS = 6
 CAP = 2
+LANES = 128
 TILE = 8
 MESH = pl.DeviceIdType.MESH
 
 
-def advance(v, drive, above_ok, below_ok):
-    rows, width = v.shape
-    v = zero_outside(v, above_ok, below_ok)
-    for _ in range(STEPS):
-        east = pltpu.roll(v, width - 1, 1)
-        west = pltpu.roll(v, 1, 1)
-        north = pltpu.roll(v, rows - 1, 0)
-        south = pltpu.roll(v, 1, 0)
-        v = (
-            v * (0.4 - 0.05 * (east - west))
-            + (0.15 * (east + west) + drive)
-            + (0.05 * north + 0.25 * south)
-        )
-        v = zero_outside(v, above_ok, below_ok)
-    return v
-
-
-def zero_outside(v, above_ok, below_ok):
-    if above_ok is not None:
-        v = jnp.concatenate([jnp.where(above_ok, v[:TILE], 0.0), v[TILE:]], axis=0)
-    if below_ok is not None:
-        v = jnp.concatenate([v[:-TILE], jnp.where(below_ok, v[-TILE:], 0.0)], axis=0)
-    return v
-
-
-def window(low, mid, high, pick, start, rows):
-    extent = mid.shape[-2]
-    begin, end = start - TILE, start + rows + TILE
-    parts = []
-    if begin < 0:
-        parts.append(low[pick + (slice(None), slice(None))])
-    parts.append(mid[pick + (slice(max(begin, 0), min(end, extent)), slice(None))])
-    if end > extent:
-        parts.append(high[pick + (slice(None), slice(None))])
-    return jnp.concatenate(parts, axis=0) if len(parts) > 1 else parts[0]
+SCALE = 0.05
+
+
+def step_rows(c, n, s, drive):
+    width = c.shape[-1]
+    east = pltpu.roll(c, width - 1, c.ndim - 1)
+    west = pltpu.roll(c, 1, c.ndim - 1)
+    return (c * (0.4 - (east - west)) + 0.15 * (east + west)) + ((0.05 * n + 0.25 * s) + drive)
 
 
 def kernel(
     bands, groups, chunks, jobs1, jobs2,
     state, forcing, taper, chosen, picks, out,
-    first, resampled,
+    first, resampled, ping, pong, drive, weight,
     s_lo, s_hi, f_lo, f_hi, t_lo, t_hi, r_lo, r_hi,
     halo_send, halo_recv, send_sem, recv_sem, own_sem,
     *buffers,
@@ -63,7 +37,7 @@
     sends, recvs = buffers[:count], buffers[count:]
     band = lax.axis_index("band")
     me = lax.axis_index("pgroup")
-    per_dev, extent, width = state.shape
+    per_dev, extent, width = state.shape[0], state.shape[1] * TILE, state.shape[2] * LANES
     has_low, has_high = band > 0, band < bands - 1
     up, down = lax.rem(band + 1, bands), lax.rem(band + bands - 1, bands)
 
@@ -82,14 +56,17 @@
         pl.semaphore_signal(barrier, inc=1, device_id={"band": up}, device_id_type=MESH)
 
     def halo(index, src, low, high):
-        lead = (slice(None),) * (len(src.shape) - 2)
+        if len(src.shape) == 5:
+            last, start = (slice(None), slice(src.shape[1] - 1, None)), (slice(None), slice(0, 1))
+        else:
+            last, start = (slice(extent - TILE, extent),), (slice(0, TILE),)
         upward = pltpu.make_async_remote_copy(
-            src_ref=src.at[lead + (slice(extent - TILE, extent),)], dst_ref=low,
+            src_ref=src.at[last], dst_ref=low,
             send_sem=halo_send.at[2 * index], recv_sem=halo_recv.at[2 * index],
             device_id={"band": up}, device_id_type=MESH,
         )
         downward = pltpu.make_async_remote_copy(
-            src_ref=src.at[lead + (slice(0, TILE),)], dst_ref=high,
+            src_ref=src.at[start], dst_ref=high,
             send_sem=halo_send.at[2 * index + 1], recv_sem=halo_recv.at[2 * index + 1],
             device_id={"band": down}, device_id_type=MESH,
         )
@@ -112,48 +89,128 @@
         for ref in (s_hi, f_hi, t_hi, r_hi):
             ref[...] = jnp.zeros_like(ref)
 
-    def bounds(start, rows):
-        return (
-            has_low if start < TILE else None,
-            has_high if start + rows + TILE > extent else None,
+    packs = per_dev // TILE
+
+    def rows_of(ref, pack, row):
+        flat, places, stride = lines(ref, pack, row)
+        return jnp.concatenate(
+            [flat[pl.ds(place, TILE, stride=stride), :] for place in places], axis=1
         )
 
+    def lines(ref, pack, row):
+        blocks = ref.shape[2]
+        per = ref.shape[1] * blocks * TILE
+        places = [
+            pack * (TILE * per) + ((row // TILE) * blocks + b) * TILE + row % TILE
+            for b in range(blocks)
+        ]
+        return ref.reshape(per_dev * per, LANES), places, per
+
+    def piece(low, mid, high, row):
+        if row < 0:
+            return low, row + TILE
+        if row >= extent:
+            return high, row - extent
+        return mid, row
+
+    def fill(low, high):
+        for row in range(low, high):
+            ref, at = piece(f_lo, forcing, f_hi, row)
+            line = SCALE * ref[pl.ds(at, 1), :]
+            drive[row + TILE] = jnp.broadcast_to(line, (TILE, width))
+            ref, at = piece(t_lo, taper, t_hi, row)
+            kind = jnp.broadcast_to(ref[pl.ds(at, 1), :], (TILE, ref.shape[1])) + 1.0
+            near, far = jnp.exp(-0.2 * kind), jnp.exp(-0.8 * kind)
+            scale = 1.0 / (1.0 + 2.0 * near + 2.0 * far)
+            weight[0, row + TILE] = scale
+            weight[1, row + TILE] = near * scale
+            weight[2, row + TILE] = far * scale
+
+    def clear(ref, low, high):
+        if low < 0:
+
+            @pl.when(jnp.logical_not(has_low))
+            def _():
+                ref[:, TILE - 1] = jnp.zeros((packs, TILE, width), jnp.float32)
+
+        if high > extent:
+
+            @pl.when(jnp.logical_not(has_high))
+            def _():
+                ref[:, TILE + extent] = jnp.zeros((packs, TILE, width), jnp.float32)
+
+    def sweep(start, rows, finish):
+        source, target = ping, pong
+        for step in range(STEPS):
+            margin = STEPS - 1 - step
+            low, high = start - margin, start + rows + margin
+            parts = 2
+            size = (high - low) // parts
+
+            def body(i, carry, low=low, size=size, source=source, target=target, last=margin == 0):
+                pack, part = i // parts, i % parts
+                at = low + TILE + part * size
+                u = step_rows(
+                    source[pack, pl.ds(at, size)],
+                    source[pack, pl.ds(at + 1, size)],
+                    source[pack, pl.ds(at - 1, size)],
+                    drive[pl.ds(at, size)],
+                )
+                if last:
+                    for r in range(size):
+                        finish(pack, at - TILE + r, u[r])
+                else:
+                    target[pack, pl.ds(at, size)] = u
+                return carry
+
+            lax.fori_loop(0, packs * parts, body, 0)
+            if margin:
+                clear(target, low, high)
+            source, target = target, source
+
+    def put(ref, factor):
+        def finish(pack, row, value):
+            if factor is not None:
+                value = value * factor
+            flat, places, stride = lines(ref, pack, row)
+            for b, place in enumerate(places):
+                flat[pl.ds(place, TILE, stride=stride), :] = value[:, b * LANES : (b + 1) * LANES]
+
+        return finish
+
     def before(start, rows):
-        above_ok, below_ok = bounds(start, rows)
-
-        def body(k, carry):
-            v = window(s_lo, state, s_hi, (k,), start, rows)
-            drive = window(f_lo, forcing, f_hi, (), start, rows)
-            v = advance(v, drive, above_ok, below_ok)
-            first[k, pl.ds(start, rows), :] = v[TILE : TILE + rows]
+        def load(pack, carry):
+            for row in range(start - STEPS, start + rows + STEPS):
+                ref, at = piece(s_lo, state, s_hi, row)
+                ping[pack, row + TILE] = SCALE * rows_of(ref, pack, at)
             return carry
 
-        lax.fori_loop(0, per_dev, body, 0)
+        lax.fori_loop(0, packs, load, 0)
+        sweep(start, rows, put(first, None))
 
     def after(start, rows):
-        above_ok, below_ok = bounds(start, rows)
-        kind = window(t_lo, taper, t_hi, (), start, rows) + 1.0
-        near, far = jnp.exp(-0.2 * kind), jnp.exp(-0.8 * kind)
-        scale = 1.0 / (1.0 + 2.0 * near + 2.0 * far)
+        low, high = start - STEPS, start + rows + STEPS
         repeat = width // taper.shape[1]
-        w0, w1, w2 = (
-            jnp.concatenate([w] * repeat, axis=1) for w in (scale, near * scale, far * scale)
-        )
-
-        def body(k, carry):
-            v = window(r_lo, resampled, r_hi, (k,), start, rows)
-            full = v.shape[0]
-            drive = window(f_lo, forcing, f_hi, (), start, rows)
-            v = (
-                w0 * v
-                + w1 * (pltpu.roll(v, 1, 0) + pltpu.roll(v, full - 1, 0))
-                + w2 * (pltpu.roll(v, 2, 0) + pltpu.roll(v, full - 2, 0))
-            )
-            v = advance(v, drive, above_ok, below_ok)
-            out[k, pl.ds(start, rows), :] = v[TILE : TILE + rows]
+
+        def load(pack, carry):
+            near = []
+            for row in range(low - 2, high + 2):
+                ref, at = piece(r_lo, resampled, r_hi, row)
+                near.append(rows_of(ref, pack, at))
+            for i, row in enumerate(range(low, high)):
+                w0, w1, w2 = (
+                    jnp.concatenate([weight[j, row + TILE]] * repeat, axis=1) for j in range(3)
+                )
+                ping[pack, row + TILE] = (
+                    w0 * near[i + 2]
+                    + w1 * (near[i + 1] + near[i + 3])
+                    + w2 * (near[i] + near[i + 4])
+                )
             return carry
 
-        lax.fori_loop(0, per_dev, body, 0)
+        lax.fori_loop(0, packs, load, 0)
+        clear(ping, low, high)
+        sweep(start, rows, put(out, 1.0 / SCALE))
 
     shifts = sorted(range(1, groups), key=lambda i: -min(i, groups - i))
 
@@ -173,7 +230,8 @@
         own = pltpu.make_async_copy(sends[index].at[me], recvs[index].at[me], own_sem.at[index])
         return copies, own
 
-    upper = lax.broadcasted_iota(jnp.int32, (TILE, width), 0) < PATCH_ROWS
+    blocks = width // LANES
+    upper = lax.broadcasted_iota(jnp.int32, (blocks, TILE, LANES), 1) < PATCH_ROWS
 
     def gather(index):
         base, tiles = chunks[index]
@@ -181,11 +239,12 @@
 
         def body(g, carry):
             for j in range(tiles):
-                rows = pl.ds((base + j) * TILE, TILE)
                 for slot in range(CAP):
                     at = ((2 * (base + j)) * groups + g) * CAP + slot
                     even, odd = chosen[at], chosen[at + groups * CAP]
-                    send[g, j, slot] = jnp.where(upper, first[even, rows, :], first[odd, rows, :])
+                    send[g, j, slot] = jnp.where(
+                        upper, first[even, base + j], first[odd, base + j]
+                    )
             return carry
 
         lax.fori_loop(0, groups, body, 0)
@@ -199,11 +258,12 @@
                 at = ((2 * (base + j)) * per_dev + k) * 2
                 even = recv[picks[at], j, picks[at + 1]]
                 odd = recv[picks[at + 2 * per_dev], j, picks[at + 2 * per_dev + 1]]
-                resampled[k, pl.ds((base + j) * TILE, TILE), :] = jnp.where(upper, even, odd)
+                resampled[k, base + j] = jnp.where(upper, even, odd)
             return carry
 
         lax.fori_loop(0, per_dev, body, 0)
 
+    fill(0, extent)
     plans = [exchange(index) for index in range(count)]
     for index in range(count):
         for start, rows in jobs1[index]:
@@ -240,6 +300,9 @@
                 for _, downward in edges:
                     downward.wait_recv()
 
+            fill(-TILE, 0)
+            fill(extent, extent + TILE)
+
     for index in range(count):
         copies, own = plans[index]
         for copy in copies:
@@ -296,7 +359,9 @@
     patch_dev = extent // PATCH_ROWS
     bands, groups = lax.axis_size("band"), lax.axis_size("pgroup")
     me = lax.axis_index("pgroup")
-    lanes = 128
+    lanes = LANES
+    blocks, row_tiles = width // lanes, extent // TILE
+    state = state.reshape(per_dev, row_tiles, TILE, blocks, lanes).transpose(0, 1, 3, 2, 4)
 
     table = parents.reshape(patch_dev, groups, per_dev)
     within = table - me * per_dev
@@ -318,16 +383,16 @@
     jobs2 = [
         [],
         [],
-        [(0, part), (part, part - TILE), (4 * part - TILE, TILE)],
+        [(0, 2 * part - TILE), (4 * part - TILE, TILE)],
         [(2 * part - TILE, part), (3 * part - TILE, part)],
     ]
     f32 = jnp.float32
-    edge = (per_dev, TILE, width)
+    edge = (per_dev, 1, blocks, TILE, lanes)
     buffers = [
-        pltpu.VMEM((groups, tiles, CAP, TILE, width), f32) for _, tiles in chunks
+        pltpu.VMEM((groups, tiles, CAP, blocks, TILE, lanes), f32) for _, tiles in chunks
     ]
     vmem, smem = pl.BlockSpec(memory_space=pltpu.VMEM), pl.BlockSpec(memory_space=pltpu.SMEM)
-    return pl.pallas_call(
+    out = pl.pallas_call(
         functools.partial(kernel, bands, groups, chunks, jobs1, jobs2),
         out_shape=jax.ShapeDtypeStruct(state.shape, f32),
         in_specs=[vmem, vmem, vmem, smem, smem],
@@ -335,6 +400,10 @@
         scratch_shapes=[
             pltpu.VMEM(state.shape, f32),
             pltpu.VMEM(state.shape, f32),
+            pltpu.VMEM((per_dev // TILE, extent + 2 * TILE, TILE, width), f32),
+            pltpu.VMEM((per_dev // TILE, extent + 2 * TILE, TILE, width), f32),
+            pltpu.VMEM((extent + 2 * TILE, TILE, width), f32),
+            pltpu.VMEM((3, extent + 2 * TILE, TILE, lanes), f32),
             pltpu.VMEM(edge, f32),
             pltpu.VMEM(edge, f32),
             pltpu.VMEM((TILE, width), f32),
@@ -356,6 +425,7 @@
         ),
         name="filter_step",
     )(state, forcing, taper, chosen, picks)
+    return out.transpose(0, 1, 3, 2, 4).reshape(per_dev, extent, width)
 
 
 def solution(mesh):

time: 112 us -> 84.6 us (0.76)
  Pallas kernels: 103 us -> 75.1 us
    pallas_call x1, Pallas kernels: 103 us -> 75.1 us  [on_device(): pl.pallas_call(functools.partial(kernel, bands, groups, chunks, jobs1, jo...]
where the time goes in v1:
time: 84.6 us; the launch traced here: 83.5 us
  Pallas kernels  75.1 us (89%)
  local copies, waits for them, and re-layouts  6.5 us (8%)
  other arithmetic  1.82 us (2%)
    pallas_call x1, Pallas kernels, on_device(): pl.pallas_call(functools.partial(kernel, bands, groups, chunks, jobs1, jo...  75.1 us
    unnamed x1, local copies, waits for them, and re-layouts  3.14 us

profile of v1, /device:TPU:14, one launch (start us, length us, event | category | flops | bytes accessed | tf_op | source)
XLA Modules:
  0.0 83.5 jit_solution(3037298599323823138)
XLA Ops:
  0.0 0.7 convert_element_type.16
  0.7 0.7 broadcast_in_dim.7.taper
  1.4 0.8 reshape.102
  2.1 0.1 and_select_fusion
  2.2 0.6 select_reduce_fusion.1
  2.8 0.1 copy.14
  2.9 0.1 copy.15
  3.0 0.5 and_reduce_fusion
  3.5 0.1 copy.16
  3.6 0.7 reshape.103.chosen
  4.3 0.2 copy.17
  4.5 0.7 reshape.104.picks
  5.2 75.1 %filter_step.1 = f32[16,8,4,8,128]{4,3,2,1,0:T(8,128)} custom-call(f32[16,8,4,8,128]{4,3,2,1,0:T(8,128)} %bitcast.14, f32[64,512]{1,0:T(8,128)} %forcing.1, f32[64,128]{1,0:T(8,128)} %broadcast_in_dim.7.taper, s32[256]{0:T(256)} %reshape.103.chosen, s32[512]{0:T(512)} %reshape.104.picks), custom_call_target="tpu_custom_call" | custom-call | tf_op jit(solution)/shard_map/filter_step/pallas_call | solution.py:395
  80.4 3.1 %copy.19 = f32[16,64,512]{2,1,0:T(8,128)} copy(f32[16,64,512]{2,1,0:T(8,128)} %bitcast.13) | data formatting | bytes 4194304
  (5 shorter events, 0.0 us)

commit v2 on v1

--- a/solution.py
+++ b/solution.py
@@ -27,7 +27,7 @@
 
 def kernel(
     bands, groups, chunks, jobs1, jobs2,
-    state, forcing, taper, chosen, picks, out,
+    state, forcing, taper, least, most, source, rank, out,
     first, resampled, ping, pong, drive, weight,
     s_lo, s_hi, f_lo, f_hi, t_lo, t_hi, r_lo, r_hi,
     halo_send, halo_recv, send_sem, recv_sem, own_sem,
@@ -113,11 +113,14 @@
             return high, row - extent
         return mid, row
 
-    def fill(low, high):
+    def fill_drive(low, high):
         for row in range(low, high):
             ref, at = piece(f_lo, forcing, f_hi, row)
             line = SCALE * ref[pl.ds(at, 1), :]
             drive[row + TILE] = jnp.broadcast_to(line, (TILE, width))
+
+    def fill_weight(low, high):
+        for row in range(low, high):
             ref, at = piece(t_lo, taper, t_hi, row)
             kind = jnp.broadcast_to(ref[pl.ds(at, 1), :], (TILE, ref.shape[1])) + 1.0
             near, far = jnp.exp(-0.2 * kind), jnp.exp(-0.8 * kind)
@@ -144,7 +147,7 @@
         for step in range(STEPS):
             margin = STEPS - 1 - step
             low, high = start - margin, start + rows + margin
-            parts = 2
+            parts = 1
             size = (high - low) // parts
 
             def body(i, carry, low=low, size=size, source=source, target=target, last=margin == 0):
@@ -210,7 +213,7 @@
 
         lax.fori_loop(0, packs, load, 0)
         clear(ping, low, high)
-        sweep(start, rows, put(out, 1.0 / SCALE))
+        sweep(start, rows, put(out, None))
 
     shifts = sorted(range(1, groups), key=lambda i: -min(i, groups - i))
 
@@ -239,9 +242,8 @@
 
         def body(g, carry):
             for j in range(tiles):
-                for slot in range(CAP):
-                    at = ((2 * (base + j)) * groups + g) * CAP + slot
-                    even, odd = chosen[at], chosen[at + groups * CAP]
+                for slot, table in enumerate((least, most)):
+                    even, odd = table[2 * (base + j), g], table[2 * (base + j) + 1, g]
                     send[g, j, slot] = jnp.where(
                         upper, first[even, base + j], first[odd, base + j]
                     )
@@ -255,15 +257,15 @@
 
         def body(k, carry):
             for j in range(tiles):
-                at = ((2 * (base + j)) * per_dev + k) * 2
-                even = recv[picks[at], j, picks[at + 1]]
-                odd = recv[picks[at + 2 * per_dev], j, picks[at + 2 * per_dev + 1]]
+                at = 2 * (base + j)
+                even = recv[source[at, k], j, rank[at, k]]
+                odd = recv[source[at + 1, k], j, rank[at + 1, k]]
                 resampled[k, base + j] = jnp.where(upper, even, odd)
             return carry
 
         lax.fori_loop(0, per_dev, body, 0)
 
-    fill(0, extent)
+    fill_drive(0, extent)
     plans = [exchange(index) for index in range(count)]
     for index in range(count):
         for start, rows in jobs1[index]:
@@ -288,7 +290,7 @@
         for copy in copies:
             copy.start()
         own.start()
-        if index == 0:
+        if index == 1:
 
             @pl.when(has_low)
             def _():
@@ -300,8 +302,9 @@
                 for _, downward in edges:
                     downward.wait_recv()
 
-            fill(-TILE, 0)
-            fill(extent, extent + TILE)
+            fill_drive(-TILE, 0)
+            fill_drive(extent, extent + TILE)
+            fill_weight(-TILE, extent + TILE)
 
     for index in range(count):
         copies, own = plans[index]
@@ -368,23 +371,30 @@
     mine = (within >= 0) & (within < per_dev)
     least = jnp.min(jnp.where(mine, within, per_dev - 1), axis=2)
     most = jnp.max(jnp.where(mine, within, 0), axis=2)
-    chosen = jnp.stack([least, most], axis=2).reshape(-1)
     own = lax.dynamic_index_in_dim(table, me, 1, keepdims=False)
     source = own // per_dev
     other = (source[:, :, None] == source[:, None, :]) & (own[:, None, :] < own[:, :, None])
     rank = jnp.any(other, axis=2).astype(jnp.int32)
-    picks = jnp.stack([source, rank], axis=2).reshape(-1)
     taper = jnp.broadcast_to(taper_index.astype(jnp.float32)[:, None], (extent, lanes))
 
     quarter = extent // TILE // 4
     part = quarter * TILE
-    chunks = [(quarter, quarter), (0, quarter), (3 * quarter, quarter), (2 * quarter, quarter)]
-    jobs1 = [[(base * TILE, part)] for base, _ in chunks]
+    chunks = [
+        (2 * quarter - 1, 1),
+        (quarter, quarter - 1),
+        (0, quarter),
+        (3 * quarter, quarter),
+        (2 * quarter, quarter - 1),
+        (3 * quarter - 1, 1),
+    ]
+    jobs1 = [[(base * TILE, tiles * TILE)] for base, tiles in chunks]
     jobs2 = [
         [],
         [],
-        [(0, 2 * part - TILE), (4 * part - TILE, TILE)],
-        [(2 * part - TILE, part), (3 * part - TILE, part)],
+        [(TILE, 2 * part - 2 * TILE)],
+        [],
+        [(2 * part - TILE, part - TILE), (0, TILE), (4 * part - TILE, TILE)],
+        [(3 * part - 2 * TILE, 3 * TILE)],
     ]
     f32 = jnp.float32
     edge = (per_dev, 1, blocks, TILE, lanes)
@@ -395,7 +405,7 @@
     out = pl.pallas_call(
         functools.partial(kernel, bands, groups, chunks, jobs1, jobs2),
         out_shape=jax.ShapeDtypeStruct(state.shape, f32),
-        in_specs=[vmem, vmem, vmem, smem, smem],
+        in_specs=[vmem, vmem, vmem, smem, smem, smem, smem],
         out_specs=vmem,
         scratch_shapes=[
             pltpu.VMEM(state.shape, f32),
@@ -424,7 +434,8 @@
             collective_id=0, has_side_effects=True, vmem_limit_bytes=56 << 20
         ),
         name="filter_step",
-    )(state, forcing, taper, chosen, picks)
+    )(state, forcing, taper, least, most, source, rank)
+    out = out * (1.0 / SCALE)
     return out.transpose(0, 1, 3, 2, 4).reshape(per_dev, extent, width)
 
 

time: 84.6 us -> 78.2 us (0.924)
  the two profiles are of different devices: /device:TPU:14 before, /device:TPU:0 now
where the time goes in v2:
time: 78.2 us; the launch traced here: 77.9 us
  Pallas kernels  70.3 us (90%)
  other arithmetic  6.11 us (8%)
  local copies, waits for them, and re-layouts  1.48 us (2%)
    pallas_call x1, Pallas kernels, on_device(): pl.pallas_call(functools.partial(kernel, bands, groups, chunks, jobs1, jo...  70.3 us
    reshape x1, other arithmetic, on_device(): return out.transpose(0, 1, 3, 2, 4).reshape(per_dev, extent, width)  3.17 us

profile of v2, /device:TPU:0, one launch (start us, length us, event | category | flops | bytes accessed | tf_op | source)
XLA Modules:
  0.0 77.9 jit_solution(656014116633140975)
XLA Ops:
  0.0 0.7 convert_element_type.6
  0.7 0.7 broadcast_in_dim.7.taper
  1.4 0.8 reshape.41
  2.1 1.2 %select_reduce_fusion = (s32[16,8]{1,0:T(8,128)}, s32[16,8]{1,0:T(8,128)}) fusion(s32[16,8,16]{2,1,0:T(8,128)S(1)} %reshape.41, s32[]{:T(128)S(6)} %mul.9), kind=kLoop, calls=%fused_computation.2 | loop fusion | flops 16128 | bytes 9220 | tf_op jit(solution)/shard_map/reduce_max | solution.py:373
  3.4 0.0 copy-start
  3.4 0.5 and_reduce_fusion
  3.8 0.6 convert_element_type.7.rank
  4.5 0.0 copy-done
  4.5 70.3 %filter_step.1 = f32[16,8,4,8,128]{4,3,2,1,0:T(8,128)} custom-call(f32[16,8,4,8,128]{4,3,2,1,0:T(8,128)} %bitcast.12, f32[64,512]{1,0:T(8,128)} %forcing.1, f32[64,128]{1,0:T(8,128)} %broadcast_in_dim.7.taper, s32[16,8]{1,0:T(8,128)} %get-tuple-element.6.least, s32[16,8]{1,0:T(8,128)} %get-tuple-element.5.most, s32[16,16]{1,0:T(8,128)} %copy-done, ...), custom_call_target="tpu_custom_call" | custom-call | tf_op jit(solution)/shard_map/filter_step/pallas_call | solution.py:405
  74.8 3.2 %multiply_bitcast_fusion = f32[16,64,512]{2,1,0:T(8,128)} fusion(f32[16,8,4,8,128]{4,3,2,1,0:T(8,128)} %filter_step.1), kind=kLoop, calls=%fused_computation | loop fusion | flops 524288 | bytes 4194304 | tf_op jit(solution)/shard_map/reshape | solution.py:439
  (3 shorter events, 0.0 us)
Async XLA Ops:
  3.4 1.1 %copy-start = (s32[16,16]{1,0:T(8,128)}, s32[16,16]{1,0:T(8,128)S(1)}, u32[]{:S(2)}) copy-start(s32[16,16]{1,0:T(8,128)S(1)} %add_select_fusion.1.source) | copy-start | bytes 3076
